TPU v7x, 32 devices: a whole 2x2x4 slice. The times are simulated.
32 devices in a mesh: layer: 8 (over y, x, core), dp: 4 (over z).
Axes of the slice: x: 2, y: 2, z: 4, core: 2. Of those that a mesh axis runs over, the one named last changes fastest.
Arguments:
- resid_in: bfloat16 [4, 128, 3584], P(None, 'dp'), may hold values from -6 to 6
- resid_out: bfloat16 [4, 128, 3584], P(None, ('layer', 'dp')), may hold values from -4 to 4
- encoder: bfloat16 [2, 3584, 32768], P(None, None, ('layer', 'dp')), may hold values from -0.09375 to 0.09375
- enc_bias: float32 [2, 32768], P(None, ('layer', 'dp')), may hold values from -3 to 3
- decoder: bfloat16 [5, 32768, 3584], P(None, ('layer', 'dp')), may hold values from -0.046875 to 0.046875
- active: int32 [4, 4, 32], replicated, may hold values from 0 to 127, all different within a row
Outputs:
- recon: bfloat16 [4, 128, 3584], P(None, ('layer', 'dp'))
- grad_encoder: bfloat16 [2, 3584, 32768], P(None, None, ('layer', 'dp'))
- grad_bias: float32 [2, 32768], P(None, ('layer', 'dp'))
- grad_decoder: bfloat16 [5, 32768, 3584], P(None, ('layer', 'dp'))
Inputs may be any that keep to these rules, and one draw needn't show every extreme that they name: Row active[l, n] lists 32 different blocks of layer l, active for tokens n * 32 to (n + 1) * 32 - 1; every block number appears in at least one row of active, counting the rows of all layers together (not necessarily in a row of every layer).
All inputs are finite; a program needn't handle non-finite values.
Results may differ from a plain program's by a relative error of at most 0.0059.
Values may be sent and summed in bfloat16 or wider, within the bound.
A program may use at most 192 MiB of HBM per device.

v0:
```python
import jax
import jax.numpy as jnp
from jax import lax
from jax.sharding import PartitionSpec as P

FEAT = 16384
BLOCK = 128
LAYERS = 4


def per_device(resid_in, resid_out, encoder, enc_bias, decoder, active):
    tok_dev = resid_in.shape[1]
    model_width = resid_in.shape[2]
    local_width = encoder.shape[2]
    dp_count = lax.axis_size("dp")
    all_count = lax.axis_size("layer") * dp_count
    device_rank = lax.axis_index("layer") * dp_count + lax.axis_index("dp")
    first_column = device_rank * local_width
    fold_side = first_column // FEAT
    offset = first_column - fold_side * FEAT
    targets = lax.all_gather(resid_out, ("layer", "dp"), axis=1, tiled=True)
    layer_ids = [fold_side, LAYERS - 1 - fold_side]
    picked = jnp.stack(
        [lax.dynamic_index_in_dim(resid_in, layer_id, 0, keepdims=False) for layer_id in layer_ids]
    )
    inputs = lax.all_gather(picked, "dp", axis=1, tiled=True)
    tokens = inputs.shape[1]
    pre_acts = (
        jnp.einsum("krd,kdf->krf", inputs, encoder, preferred_element_type=jnp.float32)
        + enc_bias[:, None, :]
    )
    block_ids = offset // BLOCK + jnp.arange(local_width // BLOCK, dtype=jnp.int32)
    block_masks = []
    for layer_id in layer_ids:
        listed = lax.dynamic_index_in_dim(active, layer_id, 0, keepdims=False)
        listed_hit = jnp.any(listed[:, :, None] == block_ids[None, None, :], axis=1).astype(
            jnp.float32
        )
        spread = jnp.broadcast_to(
            listed_hit[:, None, :, None], (listed_hit.shape[0], tok_dev, listed_hit.shape[1], BLOCK)
        )
        block_masks.append(spread.reshape(tokens, local_width))
    block_keep = jnp.stack(block_masks)
    positive = jnp.maximum(pre_acts, 0.0)
    feature_codes = (block_keep * positive * positive).astype(jnp.bfloat16)
    pair_table = []
    for pair_slot in range(decoder.shape[0]):
        second = pair_slot >= LAYERS - fold_side
        pair_table.append(
            (second.astype(jnp.int32), jnp.where(second, pair_slot - 1, fold_side + pair_slot))
        )
    decoded = jnp.zeros((LAYERS, tokens, model_width), jnp.float32)
    for pair_slot in range(decoder.shape[0]):
        source_slot, target_layer = pair_table[pair_slot]
        source_codes = lax.dynamic_index_in_dim(feature_codes, source_slot, 0, keepdims=False)
        decoded_part = jnp.dot(source_codes, decoder[pair_slot], preferred_element_type=jnp.float32)
        current = lax.dynamic_index_in_dim(decoded, target_layer, 0, keepdims=False)
        decoded = lax.dynamic_update_index_in_dim(decoded, current + decoded_part, target_layer, 0)
    totals = lax.psum(decoded, ("layer", "dp"))
    share = tokens // all_count
    recon = lax.dynamic_slice_in_dim(totals, device_rank * share, share, 1).astype(jnp.bfloat16)
    errors_all = (totals - targets.astype(jnp.float32)).astype(jnp.bfloat16)
    grad_parts = []
    back_codes = jnp.zeros((2, tokens, local_width), jnp.float32)
    for pair_slot in range(decoder.shape[0]):
        source_slot, target_layer = pair_table[pair_slot]
        source_codes = lax.dynamic_index_in_dim(feature_codes, source_slot, 0, keepdims=False)
        target_errors = lax.dynamic_index_in_dim(errors_all, target_layer, 0, keepdims=False)
        grad_parts.append(
            lax.dot_general(
                source_codes,
                target_errors,
                (((0,), (0,)), ((), ())),
                preferred_element_type=jnp.float32,
            ).astype(jnp.bfloat16)
        )
        pulled = lax.dot_general(
            target_errors,
            decoder[pair_slot],
            (((1,), (1,)), ((), ())),
            preferred_element_type=jnp.float32,
        )
        current = lax.dynamic_index_in_dim(back_codes, source_slot, 0, keepdims=False)
        back_codes = lax.dynamic_update_index_in_dim(back_codes, current + pulled, source_slot, 0)
    grad_decoder = jnp.stack(grad_parts)
    back_pre = (back_codes * block_keep * (2.0 * positive)).astype(jnp.bfloat16)
    grad_encoder = jnp.einsum(
        "krd,krf->kdf", inputs, back_pre, preferred_element_type=jnp.float32
    ).astype(jnp.bfloat16)
    grad_bias = jnp.sum(back_pre.astype(jnp.float32), axis=1)
    return (recon, grad_encoder, grad_bias, grad_decoder)


def solution(mesh):
    in_specs = (
        P(None, "dp", None),
        P(None, ("layer", "dp"), None),
        P(None, None, ("layer", "dp")),
        P(None, ("layer", "dp")),
        P(None, ("layer", "dp"), None),
        P(),
    )
    out_specs = (
        P(None, ("layer", "dp"), None),
        P(None, None, ("layer", "dp")),
        P(None, ("layer", "dp")),
        P(None, ("layer", "dp"), None),
    )
    return jax.shard_map(
        per_device, mesh=mesh, in_specs=in_specs, out_specs=out_specs, check_vma=False
    )
```

profile of v0, /device:TPU:12, one launch (start us, length us, event | category | flops | bytes accessed | tf_op | source)
XLA Modules:
  0.0 402.6 jit_solution(1773918791542335406)
XLA Ops:
  7.2 0.0 copy-start.2
  7.2 0.0 all-gather.3.cloned.1.call-start
  7.3 1.1 constant_dynamic-slice_fusion.9
  8.3 0.8 pad_maximum_fusion
  9.1 0.0 all-gather.3.cloned.1.call-update
  9.2 0.0 all-reduce.2.cloned.1.call-start
  9.3 0.7 fusion.171
  10.0 0.3 compare_reduce_fusion
  10.3 0.1 broadcast_in_dim.53
  10.4 0.1 stack_reshape.6
  10.5 0.1 broadcast_in_dim.54
  10.6 0.1 stack_reshape.7
  10.9 40.6 %all-gather.3.cloned.1.call-done = bf16[2,128,3584]{2,1,0:T(8,128)(2,1)} async-done(((bf16[2,32,3584]{2,1,0:T(8,128)(2,1)}), bf16[2,128,3584]{2,1,0:T(8,128)(2,1)}) %all-gather.3.cloned.1.call-update) | async-done | bytes 1835024 | tf_op jit(solution)/shard_map/all_gather | solution.py:26
  51.5 0.0 copy-done.2
  51.5 8.0 %fusion.115 = (bf16[2,128,1024]{2,1,0:T(8,128)(2,1)S(1)}, f32[2,128,1024]{2,1,0:T(8,128)S(1)}) fusion(f32[2,128,1024]{2,1,0:T(8,128)S(1)} %constant_dynamic-update-slice_fusion, f32[2,1024]{1,0:T(2,128)S(1)} %copy-done.2, bf16[2,128,3584]{2,1,0:T(8,128)(2,1)} %all-gather.3.cloned.1.call-done, bf16[2,3584,1024]{2,1,0:T(8,128)(2,1)} %param.8), kind=kOutput, calls=%fused_computation.73 | convolution fusion | flops 1880358912 | bytes 19144704 | tf_op jit(solution)/shard_map/krd,kdf->krf/dot_general | solution.py:29
  59.5 3.9 broadcast_in_dim.52
  63.4 5.4 %fusion.33 = f32[4,128,3584]{2,1,0:T(8,128)} fusion(f32[4,128,3584]{2,1,0:T(8,128)} %broadcast_in_dim.52, s32[]{:T(128)S(6)} %select_n.104, bf16[5,1024,3584]{2,1,0:T(8,128)(2,1)} %param.10, bf16[2,128,1024]{2,1,0:T(8,128)(2,1)S(1)} %get-tuple-element.16, s32[]{:T(128)S(6)} %select_n.102), kind=kOutput, calls=%fused_computation.43 | convolution fusion | flops 939524096 | bytes 9437192 | tf_op jit(solution)/shard_map/dot_general | solution.py:56
  68.9 1.6 constant_dynamic-slice_fusion.7
  70.5 5.5 %fusion.42 = f32[4,128,3584]{2,1,0:T(8,128)} fusion(f32[4,128,3584]{2,1,0:T(8,128)} %fusion.33, s32[]{:T(128)S(6)} %select_n.106, bf16[5,1024,3584]{2,1,0:T(8,128)(2,1)} %param.10, f32[1,128,3584]{2,1,0:T(8,128)S(1)} %constant_dynamic-slice_fusion.7, bf16[2,128,1024]{2,1,0:T(8,128)(2,1)S(1)} %get-tuple-element.16, s32[]{:T(128)S(6)} %select_n.107), kind=kOutput, calls=%fused_computation.46 | convolution fusion | flops 939982848 | bytes 11272200 | tf_op jit(solution)/shard_map/dot_general | solution.py:56
  75.9 1.6 constant_dynamic-slice_fusion.6
  77.6 5.5 %fusion.51 = f32[4,128,3584]{2,1,0:T(8,128)} fusion(f32[4,128,3584]{2,1,0:T(8,128)} %fusion.42, s32[]{:T(128)S(6)} %select_n.109, bf16[5,1024,3584]{2,1,0:T(8,128)(2,1)} %param.10, f32[1,128,3584]{2,1,0:T(8,128)S(1)} %constant_dynamic-slice_fusion.6, bf16[2,128,1024]{2,1,0:T(8,128)(2,1)S(1)} %get-tuple-element.16, s32[]{:T(128)S(6)} %select_n.110), kind=kOutput, calls=%fused_computation.49 | convolution fusion | flops 939982848 | bytes 11272200 | tf_op jit(solution)/shard_map/dot_general | solution.py:56
  83.0 1.6 constant_dynamic-slice_fusion.4
  84.7 5.5 %fusion.60 = f32[4,128,3584]{2,1,0:T(8,128)} fusion(f32[4,128,3584]{2,1,0:T(8,128)} %fusion.51, s32[]{:T(128)S(6)} %select_n.112, bf16[5,1024,3584]{2,1,0:T(8,128)(2,1)} %param.10, f32[1,128,3584]{2,1,0:T(8,128)S(1)} %constant_dynamic-slice_fusion.4, bf16[2,128,1024]{2,1,0:T(8,128)(2,1)S(1)} %get-tuple-element.16, s32[]{:T(128)S(6)} %select_n.113), kind=kOutput, calls=%fused_computation.52 | convolution fusion | flops 939982848 | bytes 11272200 | tf_op jit(solution)/shard_map/dot_general | solution.py:56
  90.1 1.6 constant_dynamic-slice_fusion.3
  91.8 0.0 copy-start.1
  91.8 5.5 %fusion.69 = f32[4,128,3584]{2,1,0:T(8,128)} fusion(f32[4,128,3584]{2,1,0:T(8,128)} %fusion.60, s32[]{:T(128)S(6)} %select_n.115, bf16[5,1024,3584]{2,1,0:T(8,128)(2,1)} %param.10, f32[1,128,3584]{2,1,0:T(8,128)S(1)} %constant_dynamic-slice_fusion.3, bf16[2,128,1024]{2,1,0:T(8,128)(2,1)S(1)} %get-tuple-element.16, s32[]{:T(128)S(6)} %select_n.116), kind=kOutput, calls=%fused_computation.55 | convolution fusion | flops 939982848 | bytes 11272200 | tf_op jit(solution)/shard_map/dot_general | solution.py:56
  97.3 0.0 all-reduce.2.cloned.1.call-update
  97.3 0.2 all-gather.5.cloned.1.call-start
  97.5 0.0 copy-done.1
  97.6 0.7 copy.19
  98.2 0.0 all-gather.5.cloned.1.call-update
  98.3 166.4 %all-reduce.2.cloned.1.call-done = f32[4,128,3584]{2,1,0:T(8,128)} async-done(((f32[4,128,3584]{2,1,0:T(8,128)}), f32[4,128,3584]{2,1,0:T(8,128)}) %all-reduce.2.cloned.1.call-update) | async-done | bytes 7340048 | tf_op jit(solution)/shard_map/psum | solution.py:59
  264.7 1.7 dynamic-slice_convert_fusion
  266.4 61.5 %all-gather.5.cloned.1.call-done = bf16[4,128,3584]{2,0,1:T(4,128)(2,1)} async-done(((bf16[4,4,3584]{2,0,1:T(4,128)(2,1)}), bf16[4,128,3584]{2,0,1:T(4,128)(2,1)}) %all-gather.5.cloned.1.call-update) | async-done | bytes 3670032 | tf_op jit(solution)/shard_map/all_gather | solution.py:21
  327.9 5.5 %subtract_convert_fusion = bf16[4,128,3584]{2,1,0:T(8,128)(2,1)S(1)} fusion(f32[4,128,3584]{2,1,0:T(8,128)} %all-reduce.2.cloned.1.call-done, bf16[4,128,3584]{2,0,1:T(4,128)(2,1)} %all-gather.5.cloned.1.call-done), kind=kLoop, calls=%fused_computation.31 | loop fusion | flops 5505024 | bytes 14680064 | tf_op jit(solution)/shard_map/convert_element_type | solution.py:62
  333.4 5.2 %bitcast_dynamic-update-slice_fusion.4 = bf16[5,1024,3584]{2,1,0:T(8,128)(2,1)} fusion(bf16[4,128,3584]{2,1,0:T(8,128)(2,1)S(1)} %subtract_convert_fusion, s32[]{:T(128)S(6)} %select_n.104, bf16[2,128,1024]{2,1,0:T(8,128)(2,1)S(1)} %get-tuple-element.16, s32[]{:T(128)S(6)} %select_n.102), kind=kOutput, calls=%fused_computation.10 | convolution fusion | flops 943194112 | bytes 8519688 | tf_op jit(solution)/shard_map/dot_general | solution.py:70
  338.6 5.1 %bitcast_dynamic-update-slice_fusion.3 = bf16[5,1024,3584]{2,1,0:T(8,128)(2,1)} fusion(bf16[5,1024,3584]{2,1,0:T(8,128)(2,1)} %bitcast_dynamic-update-slice_fusion.4, bf16[4,128,3584]{2,1,0:T(8,128)(2,1)S(1)} %subtract_convert_fusion, s32[]{:T(128)S(6)} %select_n.106, bf16[2,128,1024]{2,1,0:T(8,128)(2,1)S(1)} %get-tuple-element.16, s32[]{:T(128)S(6)} %select_n.107), kind=kOutput, calls=%fused_computation.9 | convolution fusion | flops 943194112 | bytes 8519688 | tf_op jit(solution)/shard_map/dot_general | solution.py:70
  343.7 5.1 %bitcast_dynamic-update-slice_fusion.2 = bf16[5,1024,3584]{2,1,0:T(8,128)(2,1)} fusion(bf16[5,1024,3584]{2,1,0:T(8,128)(2,1)} %bitcast_dynamic-update-slice_fusion.3, bf16[4,128,3584]{2,1,0:T(8,128)(2,1)S(1)} %subtract_convert_fusion, s32[]{:T(128)S(6)} %select_n.109, bf16[2,128,1024]{2,1,0:T(8,128)(2,1)S(1)} %get-tuple-element.16, s32[]{:T(128)S(6)} %select_n.110), kind=kOutput, calls=%fused_computation.8 | convolution fusion | flops 943194112 | bytes 8519688 | tf_op jit(solution)/shard_map/dot_general | solution.py:70
  348.9 5.1 %bitcast_dynamic-update-slice_fusion.1 = bf16[5,1024,3584]{2,1,0:T(8,128)(2,1)} fusion(bf16[5,1024,3584]{2,1,0:T(8,128)(2,1)} %bitcast_dynamic-update-slice_fusion.2, bf16[4,128,3584]{2,1,0:T(8,128)(2,1)S(1)} %subtract_convert_fusion, s32[]{:T(128)S(6)} %select_n.112, bf16[2,128,1024]{2,1,0:T(8,128)(2,1)S(1)} %get-tuple-element.16, s32[]{:T(128)S(6)} %select_n.113), kind=kOutput, calls=%fused_computation.7 | convolution fusion | flops 943194112 | bytes 8519688 | tf_op jit(solution)/shard_map/dot_general | solution.py:70
  354.0 5.1 %bitcast_dynamic-update-slice_fusion = bf16[5,1024,3584]{2,1,0:T(8,128)(2,1)} fusion(bf16[5,1024,3584]{2,1,0:T(8,128)(2,1)} %bitcast_dynamic-update-slice_fusion.1, bf16[4,128,3584]{2,1,0:T(8,128)(2,1)S(1)} %subtract_convert_fusion, s32[]{:T(128)S(6)} %select_n.115, bf16[2,128,1024]{2,1,0:T(8,128)(2,1)S(1)} %get-tuple-element.16, s32[]{:T(128)S(6)} %select_n.116), kind=kOutput, calls=%fused_computation.6 | convolution fusion | flops 943194112 | bytes 8519688 | tf_op jit(solution)/shard_map/dot_general | solution.py:70
  359.2 0.1 broadcast.16
  359.3 5.7 %fusion.76 = f32[2,128,1024]{2,1,0:T(8,128)S(1)} fusion(f32[2,128,1024]{2,1,0:T(8,128)S(1)} %broadcast.16, s32[]{:T(128)S(6)} %select_n.102, bf16[5,1024,3584]{2,1,0:T(8,128)(2,1)} %param.10, bf16[4,128,3584]{2,1,0:T(8,128)(2,1)S(1)} %subtract_convert_fusion, s32[]{:T(128)S(6)} %select_n.104), kind=kOutput, calls=%fused_computation.60 | convolution fusion | flops 939524096 | bytes 8781832 | tf_op jit(solution)/shard_map/dot_general | solution.py:77
  365.1 5.5 %fusion.85 = f32[2,128,1024]{2,1,0:T(8,128)S(1)} fusion(f32[2,128,1024]{2,1,0:T(8,128)S(1)} %fusion.76, s32[]{:T(128)S(6)} %select_n.107, bf16[5,1024,3584]{2,1,0:T(8,128)(2,1)} %param.10, bf16[4,128,3584]{2,1,0:T(8,128)(2,1)S(1)} %subtract_convert_fusion, s32[]{:T(128)S(6)} %select_n.106, f32[1,128,1024]{2,1,0:T(8,128)S(1)} %constant_dynamic-slice_fusion.2), kind=kOutput, calls=%fused_computation.63 | convolution fusion | flops 939655168 | bytes 9306120 | tf_op jit(solution)/shard_map/dot_general | solution.py:77
  370.7 5.5 %fusion.94 = f32[2,128,1024]{2,1,0:T(8,128)S(1)} fusion(f32[2,128,1024]{2,1,0:T(8,128)S(1)} %fusion.85, s32[]{:T(128)S(6)} %select_n.110, bf16[5,1024,3584]{2,1,0:T(8,128)(2,1)} %param.10, bf16[4,128,3584]{2,1,0:T(8,128)(2,1)S(1)} %subtract_convert_fusion, s32[]{:T(128)S(6)} %select_n.109, f32[1,128,1024]{2,1,0:T(8,128)S(1)} %constant_dynamic-slice_fusion.1), kind=kOutput, calls=%fused_computation.66 | convolution fusion | flops 939655168 | bytes 9306120 | tf_op jit(solution)/shard_map/dot_general | solution.py:77
  376.3 5.5 %fusion.103 = f32[2,128,1024]{2,1,0:T(8,128)S(1)} fusion(f32[2,128,1024]{2,1,0:T(8,128)S(1)} %fusion.94, s32[]{:T(128)S(6)} %select_n.113, bf16[5,1024,3584]{2,1,0:T(8,128)(2,1)} %param.10, bf16[4,128,3584]{2,1,0:T(8,128)(2,1)S(1)} %subtract_convert_fusion, s32[]{:T(128)S(6)} %select_n.112, f32[1,128,1024]{2,1,0:T(8,128)S(1)} %constant_dynamic-slice_fusion), kind=kOutput, calls=%fused_computation.69 | convolution fusion | flops 939655168 | bytes 9306120 | tf_op jit(solution)/shard_map/dot_general | solution.py:77
  381.9 0.0 copy-start
  381.9 5.7 %fusion.112 = f32[2,128,1024]{2,1,0:T(8,128)S(1)} fusion(f32[2,128,1024]{2,1,0:T(8,128)S(1)} %fusion.103, s32[]{:T(128)S(6)} %select_n.116, bf16[5,1024,3584]{2,1,0:T(8,128)(2,1)} %param.10, bf16[4,128,3584]{2,1,0:T(8,128)(2,1)S(1)} %subtract_convert_fusion, s32[]{:T(128)S(6)} %select_n.115, f32[1,128,1024]{2,1,0:T(8,128)S(1)} %constant_dynamic-slice_fusion.5), kind=kOutput, calls=%fused_computation.72 | convolution fusion | flops 939655168 | bytes 9306120 | tf_op jit(solution)/shard_map/dot_general | solution.py:77
  387.6 1.0 convert_reduce_fusion
  388.5 0.0 copy-done
  388.5 7.6 %convolution_convert_fusion = bf16[2,3584,1024]{2,1,0:T(8,128)(2,1)} fusion(bf16[2,128,3584]{2,1,0:T(8,128)(2,1)S(1)} %copy-done, bf16[2,128,1024]{2,1,0:T(8,128)(2,1)S(1)} %get-tuple-element.11), kind=kOutput, calls=%fused_computation | convolution fusion | flops 1886388224 | bytes 17039360 | tf_op jit(solution)/shard_map/krd,krf->kdf/dot_general | solution.py:87
  (9 shorter events, 0.3 us)
Async XLA Ops:
  7.2 44.3 %copy-start.2 = (f32[2,1024]{1,0:T(2,128)S(1)}, f32[2,1024]{1,0:T(2,128)}, u32[]{:S(2)}) copy-start(f32[2,1024]{1,0:T(2,128)} %param.9) | copy-start | bytes 24580
  7.2 44.3 %all-gather.3.cloned.1.call-start = ((), (), s32[]{:S(2)}) async-start(), calls=%async_computation | async-start | bytes 2293760 | tf_op jit(solution)/shard_map/all_gather | solution.py:26
  9.2 255.5 %all-reduce.2.cloned.1.call-start = ((), (), s32[]{:S(2)}) async-start(), calls=%async_computation.1 | async-start | bytes 14680064 | tf_op jit(solution)/shard_map/psum | solution.py:59
  91.8 5.8 %copy-start.1 = (bf16[4,4,3584]{2,1,0:T(4,128)(2,1)S(1)}, bf16[4,4,3584]{2,1,0:T(4,128)(2,1)}, u32[]{:S(2)}) copy-start(bf16[4,4,3584]{2,1,0:T(4,128)(2,1)} %param.7) | copy-start | bytes 344068
  97.3 230.6 %all-gather.5.cloned.1.call-start = ((), (), s32[]{:S(2)}) async-start(), calls=%async_computation.2 | async-start | bytes 3784704 | tf_op jit(solution)/shard_map/all_gather | solution.py:21
  381.9 6.6 %copy-start = (bf16[2,128,3584]{2,1,0:T(8,128)(2,1)S(1)}, bf16[2,128,3584]{2,1,0:T(8,128)(2,1)}, u32[]{:S(2)}) copy-start(bf16[2,128,3584]{2,1,0:T(8,128)(2,1)} %all-gather.3.cloned.1.call-done) | copy-start | bytes 5505028
Sparse Core Ops, SparseCore 0:
  10.1 41.3 all-gather.2
  97.4 167.2 all-reduce.1
  268.1 59.8 all-gather.4
where the time goes:
time: 406 us; the launch traced here: 403 us
  waiting for transfers between devices  269 us (66%)
  matrix products  96.6 us (24%)
  local copies, waits for them, and re-layouts  15.4 us (4%)
  between operations  14.1 us (3%)
  other arithmetic  7.55 us (2%)
    psum x1, waiting for transfers between devices, per_device(): totals = lax.psum(decoded, ('layer', 'dp'))  166 us
    all_gather x1, waiting for transfers between devices, per_device(): targets = lax.all_gather(resid_out, ('layer', 'dp'), axis=1, tiled=True)  61.5 us
    all_gather x1, waiting for transfers between devices, per_device(): inputs = lax.all_gather(picked, 'dp', axis=1, tiled=True)  40.6 us
    dot_general x5, matrix products, per_device(): lax.dot_general(target_errors, decoder[pair_slot], (((1,), (1,)), ((), ()...  28 us
    dot_general x5, matrix products, per_device(): jnp.dot(source_codes, decoder[pair_slot], preferred_element_type=jnp.floa...  27.3 us
    dot_general x5, matrix products, per_device(): lax.dot_general(source_codes, target_errors, (((0,), (0,)), ((), ())), pr...  25.7 us
  transfers between devices with their start and end apart: 3, of which 3 were waited for; matrix products, arithmetic and copies ran while one was open for 1% of the time, Pallas kernels for 0%

commit v1 on v0

--- a/solution.py
+++ b/solution.py
@@ -1,29 +1,390 @@
+import functools
+
 import jax
 import jax.numpy as jnp
 from jax import lax
+from jax.experimental import pallas as pl
+from jax.experimental.pallas import tpu as pltpu
 from jax.sharding import PartitionSpec as P
 
 FEAT = 16384
 BLOCK = 128
 LAYERS = 4
+MESH = pl.DeviceIdType.MESH
+VMEM_LIMIT = 63 * 1000 * 1000
+
+
+def remote(src, dst, send_sem, recv_sem, layer, dp):
+    return pltpu.make_async_remote_copy(
+        src_ref=src,
+        dst_ref=dst,
+        send_sem=send_sem,
+        recv_sem=recv_sem,
+        device_id=(layer, dp),
+        device_id_type=MESH,
+    )
+
+
+def greet(layer, dp, dp_count, bits):
+    barrier = pltpu.get_barrier_semaphore()
+    for hop in range(1, dp_count):
+        pl.semaphore_signal(
+            barrier, inc=1, device_id=(layer, lax.rem(dp + hop, dp_count)), device_id_type=MESH
+        )
+    for bit in bits:
+        pl.semaphore_signal(
+            barrier, inc=1, device_id=(flip(layer, bit), dp), device_id_type=MESH
+        )
+    return barrier, dp_count - 1 + len(bits)
+
+
+def bit_of(value, bit):
+    return (value // (1 << bit)) % 2
+
+
+def flip(value, bit):
+    return value + (1 - 2 * bit_of(value, bit)) * (1 << bit)
+
+
+def spread_bits(base, bits, count):
+    for place, bit in enumerate(bits):
+        base = base + (((count >> place) & 1) - bit_of(base, bit)) * (1 << bit)
+    return base
+
+
+def gather_kernel(layer_count, dp_count, x_ref, g_ref, hold, send_sem, recv_sem, near_sem, out_sem):
+    layer, dp = lax.axis_index("layer"), lax.axis_index("dp")
+    group = layer_count // 2
+    halves = x_ref.shape[1]
+    nbits = group.bit_length() - 1
+    side = layer // group
+    bits = list(range(nbits - 1, -1, -1))
+    barrier, greeted = greet(layer, dp, dp_count, bits)
+    mine = layer % group
+    near = []
+    for slot in range(2):
+        layer_id = side + slot * (LAYERS - 1 - 2 * side)
+        copy = pltpu.make_async_copy(
+            x_ref.at[layer_id], hold.at[slot, dp], near_sem.at[slot]
+        )
+        copy.start()
+        near.append(copy)
+    pl.semaphore_wait(barrier, greeted)
+
+    def piece(ref, source, index):
+        return ref.at[index // halves, source, index % halves]
+
+    copies = {}
+    my_slot = mine // halves
+    own = x_ref.at[side + my_slot * (LAYERS - 1 - 2 * side), mine % halves]
+    for hop in range(1, dp_count):
+        copies[hop, 0] = remote(
+            own, piece(hold, dp, mine), send_sem.at[hop, 0], recv_sem.at[hop, 0],
+            layer, lax.rem(dp + hop, dp_count),
+        )
+        copies[hop, 0].start()
+    for step, bit in enumerate(bits):
+        for hop in range(1, dp_count):
+            source = lax.rem(dp + dp_count - hop, dp_count)
+            arrived = [0] if step == 0 else range(1 << (step - 1), 1 << step)
+            for index in arrived:
+                copies[hop, index].wait_recv()
+            for count in range(1 << step):
+                index = spread_bits(mine, bits[:step], count)
+                slot = (1 << step) + count
+                block = piece(hold, source, index)
+                copies[hop, slot] = remote(
+                    block, block, send_sem.at[hop, slot], recv_sem.at[hop, slot],
+                    flip(layer, bit), dp,
+                )
+                copies[hop, slot].start()
+    for hop in range(1, dp_count):
+        for index in range(group // 2, group):
+            copies[hop, index].wait_recv()
+    for copy in near:
+        copy.wait()
+    out = pltpu.make_async_copy(hold, g_ref, out_sem)
+    out.start()
+    for copy in copies.values():
+        copy.wait_send()
+    out.wait()
+
+
+def gather_inputs(resid_in, layer_count, dp_count):
+    layers, tok_dev, width = resid_in.shape
+    group = layer_count // 2
+    halves = group // 2
+    rows = tok_dev // halves
+    x = resid_in.reshape(layers, halves, rows, width)
+    shape = (2, dp_count, halves, rows, width)
+    out = pl.pallas_call(
+        functools.partial(gather_kernel, layer_count, dp_count),
+        out_shape=jax.ShapeDtypeStruct(shape, resid_in.dtype),
+        in_specs=[pl.BlockSpec(memory_space=pltpu.VMEM)],
+        out_specs=pl.BlockSpec(memory_space=pl.ANY),
+        scratch_shapes=[
+            pltpu.VMEM(shape, resid_in.dtype),
+            pltpu.SemaphoreType.DMA((dp_count, group)),
+            pltpu.SemaphoreType.DMA((dp_count, group)),
+            pltpu.SemaphoreType.DMA((2,)),
+            pltpu.SemaphoreType.DMA,
+        ],
+        compiler_params=pltpu.CompilerParams(
+            collective_id=0, has_side_effects=True, vmem_limit_bytes=32 * 1000 * 1000
+        ),
+        name="gather_inputs",
+    )(x)
+    return out.reshape(2, dp_count * tok_dev, width)
+
+
+def exchange_kernel(
+    layer_count, dp_count, codes_ref, dec_ref, target_ref, recon_ref, err_out,
+    weights, part, arrivals, err, zsend, zrecv, zall, acc,
+    load_sem, rs_send, rs_recv, z_send, z_recv, g_send, g_recv, ag_send, ag_recv, out_sem,
+):
+    layer, dp = lax.axis_index("layer"), lax.axis_index("dp")
+    nbits = layer_count.bit_length() - 1
+    side = layer // (layer_count // 2)
+    pairs, width = dec_ref.shape[0], dec_ref.shape[2]
+    rows = part.shape[2]
+    share = target_ref.shape[1]
+    f32, bf16 = jnp.float32, jnp.bfloat16
+    loads = []
+    for pair in range(pairs):
+        loads.append(pltpu.make_async_copy(dec_ref.at[pair], weights.at[pair], load_sem.at[pair]))
+        loads[-1].start()
+    barrier, greeted = greet(layer, dp, dp_count, range(nbits))
+    tile = 512 if width % 512 == 0 else 128
+    orders = []
+    for target in range(LAYERS):
+        upper = list(range(nbits - 1, 0, -1))
+        orders.append([0] + (upper if target % 2 else upper[::-1]))
+    copies = {}
+
+    def add_pair(slot, pair, fresh):
+        def body(step, carry):
+            columns = pl.ds(pl.multiple_of(step * tile, tile), tile)
+            value = jnp.dot(
+                codes_ref[slot], weights[pair, :, columns], preferred_element_type=f32
+            )
+            if fresh:
+                acc[:, columns] = value
+            else:
+                acc[:, columns] += value
+            return carry
+
+        lax.fori_loop(0, width // tile, body, 0)
+
+    def wait_load(pair):
+        loads[pair].wait()
+
+    def decode(target):
+        has_first = (target >= side) if target == 0 else None
+
+        def first():
+            add_pair(0, target - side, True)
+
+        if target == 0:
+            pl.when(side == 0)(first)
+
+            @pl.when(side != 0)
+            def _():
+                acc[...] = jnp.zeros_like(acc)
+        else:
+            first()
+        if target >= LAYERS - 2:
+            def second():
+                add_pair(1, target + 1, False)
+
+            if target == LAYERS - 2:
+                pl.when(side == 1)(second)
+            else:
+                second()
+        part[target] = acc[...].reshape(part.shape[1:]).astype(bf16)
+
+    def halve_send(target, stage):
+        order = orders[target]
+        bit = order[stage]
+        partner = flip(layer, bit)
+        rest = order[stage + 1:]
+        for count in range(1 << len(rest)):
+            block = spread_bits(partner, rest, count)
+            slot = (1 << len(rest)) - 1 + count
+            copy = remote(
+                part.at[target, block], arrivals.at[target, slot],
+                rs_send.at[target, slot], rs_recv.at[target, slot], partner, dp,
+            )
+            copy.start()
+            copies["rs", target, slot] = copy
+
+    def halve_take(target, stage):
+        order = orders[target]
+        rest = order[stage + 1:]
+        for count in range(1 << len(rest)):
+            slot = (1 << len(rest)) - 1 + count
+            copies["rs", target, slot].wait_recv()
+            block = spread_bits(layer, rest, count)
+            total = part[target, block].astype(f32) + arrivals[target, slot].astype(f32)
+            if stage < nbits - 1:
+                part[target, block] = total.astype(bf16)
+            else:
+                for place in range(dp_count):
+                    zsend[target, place] = total[place * share:(place + 1) * share].astype(bf16)
+
+    def peers():
+        for hop in range(1, dp_count):
+            yield hop, lax.rem(dp + hop, dp_count)
+
+    def swap_send(target):
+        for hop, peer in peers():
+            copy = remote(
+                zsend.at[target, peer], zrecv.at[target, hop],
+                z_send.at[target, hop], z_recv.at[target, hop], layer, peer,
+            )
+            copy.start()
+            copies["z", target, hop] = copy
+
+    def finish(target):
+        total = zsend[target, dp].astype(f32)
+        for hop in range(1, dp_count):
+            copies["z", target, hop].wait_recv()
+            total = total + zrecv[target, hop].astype(f32)
+        recon_ref[target] = total.astype(bf16)
+        zall[target, dp] = (total - target_ref[target].astype(f32)).astype(bf16)
+        for hop, peer in peers():
+            copy = remote(
+                zall.at[target, dp], zall.at[target, dp],
+                g_send.at[target, hop], g_recv.at[target, hop], layer, peer,
+            )
+            copy.start()
+            copies["g", target, hop] = copy
+
+    def assemble(target):
+        for hop in range(1, dp_count):
+            copies["g", target, hop].wait_recv()
+        err[target, layer] = jnp.concatenate(
+            [zall[target, place].astype(f32) for place in range(dp_count)], axis=0
+        ).astype(bf16)
+
+    def double_send(target, step):
+        order = orders[target][::-1]
+        bit = order[step]
+        for count in range(1 << step):
+            block = spread_bits(layer, order[:step], count)
+            slot = (1 << step) - 1 + count
+            copy = remote(
+                err.at[target, block], err.at[target, block],
+                ag_send.at[target, slot], ag_recv.at[target, slot], flip(layer, bit), dp,
+            )
+            copy.start()
+            copies["ag", target, slot] = copy
+
+    def double_take(target, step):
+        for count in range(1 << step):
+            copies["ag", target, (1 << step) - 1 + count].wait_recv()
+
+    def run(target, stage):
+        if stage == 0:
+            decode(target)
+            if target == 0:
+                pl.semaphore_wait(barrier, greeted)
+            halve_send(target, 0)
+        elif stage <= nbits:
+            halve_take(target, stage - 1)
+            if stage < nbits:
+                halve_send(target, stage)
+            else:
+                swap_send(target)
+        elif stage == nbits + 1:
+            finish(target)
+        elif stage == nbits + 2:
+            assemble(target)
+            double_send(target, 0)
+        else:
+            step = stage - nbits - 3
+            double_take(target, step)
+            if step < nbits - 1:
+                double_send(target, step + 1)
+            else:
+                copy = pltpu.make_async_copy(err.at[target], err_out.at[target], out_sem.at[target])
+                copy.start()
+                copies["out", target, 0] = copy
+
+    for load in loads:
+        load.wait()
+    last = 2 * nbits + 2
+    for wave in range(last + LAYERS):
+        for target in range(LAYERS - 1, -1, -1):
+            if 0 <= wave - target <= last:
+                run(target, wave - target)
+    for key, copy in copies.items():
+        if key[0] == "out":
+            copy.wait()
+        else:
+            copy.wait_send()
+
+
+def exchange(codes, decoder, targets, layer_count, dp_count):
+    tokens = codes.shape[1]
+    pairs, local_width, width = decoder.shape
+    rows = tokens // layer_count
+    share = rows // dp_count
+    bf16 = jnp.bfloat16
+    dma = pltpu.SemaphoreType.DMA
+    recon, errors = pl.pallas_call(
+        functools.partial(exchange_kernel, layer_count, dp_count),
+        out_shape=[
+            jax.ShapeDtypeStruct((LAYERS, share, width), bf16),
+            jax.ShapeDtypeStruct((LAYERS, layer_count, rows, width), bf16),
+        ],
+        in_specs=[
+            pl.BlockSpec(memory_space=pltpu.VMEM),
+            pl.BlockSpec(memory_space=pl.ANY),
+            pl.BlockSpec(memory_space=pltpu.VMEM),
+        ],
+        out_specs=[
+            pl.BlockSpec(memory_space=pltpu.VMEM),
+            pl.BlockSpec(memory_space=pl.ANY),
+        ],
+        scratch_shapes=[
+            pltpu.VMEM((pairs, local_width, width), bf16),
+            pltpu.VMEM((LAYERS, layer_count, rows, width), bf16),
+            pltpu.VMEM((LAYERS, layer_count - 1, rows, width), bf16),
+            pltpu.VMEM((LAYERS, layer_count, rows, width), bf16),
+            pltpu.VMEM((LAYERS, dp_count, share, width), bf16),
+            pltpu.VMEM((LAYERS, dp_count, share, width), bf16),
+            pltpu.VMEM((LAYERS, dp_count, share, width), bf16),
+            pltpu.VMEM((tokens, width), jnp.float32),
+            dma((pairs,)),
+            dma((LAYERS, layer_count - 1)),
+            dma((LAYERS, layer_count - 1)),
+            dma((LAYERS, dp_count)),
+            dma((LAYERS, dp_count)),
+            dma((LAYERS, dp_count)),
+            dma((LAYERS, dp_count)),
+            dma((LAYERS, layer_count - 1)),
+            dma((LAYERS, layer_count - 1)),
+            dma((LAYERS,)),
+        ],
+        compiler_params=pltpu.CompilerParams(
+            collective_id=1, has_side_effects=True, vmem_limit_bytes=VMEM_LIMIT
+        ),
+        name="decode_exchange",
+    )(codes, decoder, targets)
+    return recon, errors.reshape(LAYERS, tokens, width)
 
 
 def per_device(resid_in, resid_out, encoder, enc_bias, decoder, active):
     tok_dev = resid_in.shape[1]
-    model_width = resid_in.shape[2]
     local_width = encoder.shape[2]
+    layer_count = lax.axis_size("layer")
     dp_count = lax.axis_size("dp")
-    all_count = lax.axis_size("layer") * dp_count
     device_rank = lax.axis_index("layer") * dp_count + lax.axis_index("dp")
     first_column = device_rank * local_width
     fold_side = first_column // FEAT
     offset = first_column - fold_side * FEAT
-    targets = lax.all_gather(resid_out, ("layer", "dp"), axis=1, tiled=True)
     layer_ids = [fold_side, LAYERS - 1 - fold_side]
-    picked = jnp.stack(
-        [lax.dynamic_index_in_dim(resid_in, layer_id, 0, keepdims=False) for layer_id in layer_ids]
-    )
-    inputs = lax.all_gather(picked, "dp", axis=1, tiled=True)
+    inputs = gather_inputs(resid_in, layer_count, dp_count)
     tokens = inputs.shape[1]
     pre_acts = (
         jnp.einsum("krd,kdf->krf", inputs, encoder, preferred_element_type=jnp.float32)
@@ -43,23 +404,13 @@
     block_keep = jnp.stack(block_masks)
     positive = jnp.maximum(pre_acts, 0.0)
     feature_codes = (block_keep * positive * positive).astype(jnp.bfloat16)
+    recon, errors_all = exchange(feature_codes, decoder, resid_out, layer_count, dp_count)
     pair_table = []
     for pair_slot in range(decoder.shape[0]):
         second = pair_slot >= LAYERS - fold_side
         pair_table.append(
             (second.astype(jnp.int32), jnp.where(second, pair_slot - 1, fold_side + pair_slot))
         )
-    decoded = jnp.zeros((LAYERS, tokens, model_width), jnp.float32)
-    for pair_slot in range(decoder.shape[0]):
-        source_slot, target_layer = pair_table[pair_slot]
-        source_codes = lax.dynamic_index_in_dim(feature_codes, source_slot, 0, keepdims=False)
-        decoded_part = jnp.dot(source_codes, decoder[pair_slot], preferred_element_type=jnp.float32)
-        current = lax.dynamic_index_in_dim(decoded, target_layer, 0, keepdims=False)
-        decoded = lax.dynamic_update_index_in_dim(decoded, current + decoded_part, target_layer, 0)
-    totals = lax.psum(decoded, ("layer", "dp"))
-    share = tokens // all_count
-    recon = lax.dynamic_slice_in_dim(totals, device_rank * share, share, 1).astype(jnp.bfloat16)
-    errors_all = (totals - targets.astype(jnp.float32)).astype(jnp.bfloat16)
     grad_parts = []
     back_codes = jnp.zeros((2, tokens, local_width), jnp.float32)
     for pair_slot in range(decoder.shape[0]):

time: 406 us -> 199 us (0.49)
  waiting for transfers between devices: 269 us -> 0 us
  Pallas kernels: 0 us -> 96.4 us
  matrix products: 96.6 us -> 75.6 us
  between operations: 14.1 us -> 0.92 us
  local copies, waits for them, and re-layouts: 15.4 us -> 22.7 us
  other arithmetic: 7.55 us -> 1.26 us
    psum x1 -> x0, waiting for transfers between devices: 166 us -> none  [per_device(): totals = lax.psum(decoded, ('layer', 'dp'))]
    all_gather x2 -> x0, waiting for transfers between devices: 102 us -> none  [the longest x1 61.5 us: per_device(): targets = lax.all_gather(resid_out, ('layer', 'dp'), axis=1, tiled=True)]
    pallas_call x0 -> x2, Pallas kernels: none -> 96.4 us  [the longest x1 77.1 us: exchange(): pl.pallas_call(functools.partial(exchange_kernel, layer_count, dp_count),...]
    dot_general x5 -> x0, matrix products: 27.3 us -> none  [per_device(): jnp.dot(source_codes, decoder[pair_slot], preferred_element_type=jnp.floa...]
    unnamed x8 -> x15, local copies, waits for them, and re-layouts: 0.75 us -> 21.3 us
    dynamic_slice x5 -> x0, local copies, waits for them, and re-layouts: 7.59 us -> none  [the longest x4 6.5 us: per_device(): current = lax.dynamic_index_in_dim(decoded, target_layer, 0, keepdims=False)]
    dot_general x5, matrix products: 25.7 us -> 31.8 us  [per_device(): lax.dot_general(source_codes, target_errors, (((0,), (0,)), ((), ())), pr...]
    convert_element_type x1 -> x0, other arithmetic: 5.48 us -> none  [per_device(): errors_all = (totals - targets.astype(jnp.float32)).astype(jnp.bfloat16)]
  transfers between devices with their start and end apart: 3 -> 0, of which waited for: 3 -> 0; matrix products, arithmetic and copies ran while one was open for 1% -> 0% of each run, Pallas kernels for 0% -> 0%
where the time goes in v1:
time: 199 us; the launch traced here: 197 us
  Pallas kernels  96.4 us (48%)
  matrix products  75.6 us (38%)
  local copies, waits for them, and re-layouts  22.7 us (11%)
    pallas_call x1, Pallas kernels, exchange(): pl.pallas_call(functools.partial(exchange_kernel, layer_count, dp_count),...  77.1 us
    dot_general x5, matrix products, per_device(): lax.dot_general(source_codes, target_errors, (((0,), (0,)), ((), ())), pr...  31.8 us
    dot_general x5, matrix products, per_device(): lax.dot_general(target_errors, decoder[pair_slot], (((1,), (1,)), ((), ()...  27.9 us
    unnamed x15, local copies, waits for them, and re-layouts  21.3 us
    pallas_call x1, Pallas kernels, gather_inputs(): pl.pallas_call(functools.partial(gather_kernel, layer_count, dp_count), o...  19.3 us
    dot_general x1, matrix products, per_device(): jnp.einsum('krd,kdf->krf', inputs, encoder, preferred_element_type=jnp.fl...  8.55 us
    dot_general x1, matrix products, per_device(): jnp.einsum('krd,krf->kdf', inputs, back_pre, preferred_element_type=jnp.f...  7.31 us

profile of v1, /device:TPU:12, one launch (start us, length us, event | category | flops | bytes accessed | tf_op | source)
XLA Modules:
  0.0 196.9 jit_solution(2397874623008680418)
XLA Ops:
  0.6 0.0 copy-start.5
  0.7 0.7 fusion.99
  1.4 0.3 compare_reduce_fusion
  1.7 0.1 broadcast_in_dim.33
  1.8 0.1 stack_reshape.6
  2.0 0.1 broadcast_in_dim.34
  2.1 0.1 stack_reshape.7
  2.2 0.0 copy-start
  2.2 1.2 copy-done
  3.4 19.3 %gather_inputs.1 = bf16[2,4,2,16,3584]{4,3,2,1,0:T(8,128)(2,1)S(1)} custom-call(bf16[4,2,16,3584]{3,2,1,0:T(8,128)(2,1)S(1)} %bitcast.140), custom_call_target="tpu_custom_call" | custom-call | tf_op jit(solution)/shard_map/gather_inputs/pallas_call | solution.py:120
  22.7 0.0 copy-done.5
  22.7 8.6 %fusion.58 = (bf16[2,128,1024]{2,1,0:T(8,128)(2,1)}, f32[2,128,1024]{2,1,0:T(8,128)}) fusion(f32[2,128,1024]{2,1,0:T(8,128)S(1)} %constant_dynamic-update-slice_fusion, f32[2,1024]{1,0:T(2,128)S(1)} %copy-done.5, bf16[2,128,3584]{2,1,0:T(8,128)(2,1)S(1)} %bitcast.138, bf16[2,3584,1024]{2,1,0:T(8,128)(2,1)} %param.8), kind=kOutput, calls=%fused_computation.43 | convolution fusion | flops 1880358912 | bytes 19144704 | tf_op jit(solution)/shard_map/krd,kdf->krf/dot_general | solution.py:390
  31.2 0.0 copy-start.1
  31.3 77.1 %decode_exchange.1 = (bf16[4,4,3584]{2,1,0:T(4,128)(2,1)}, bf16[4,8,16,3584]{3,2,1,0:T(8,128)(2,1)}) custom-call(bf16[2,128,1024]{2,1,0:T(8,128)(2,1)} %get-tuple-element.22.codes_ref, bf16[5,1024,3584]{2,1,0:T(8,128)(2,1)} %dec_ref.1, bf16[4,4,3584]{2,1,0:T(4,128)(2,1)} %target_ref.1), custom_call_target="tpu_custom_call" | custom-call | tf_op jit(solution)/shard_map/decode_exchange/pallas_call | solution.py:334
  108.4 0.0 copy-done.1
  108.4 6.3 %bitcast_dynamic-update-slice_fusion.4 = bf16[5,1024,3584]{2,1,0:T(8,128)(2,1)} fusion(bf16[4,128,3584]{2,1,0:T(8,128)(2,1)} %bitcast.141, s32[]{:T(128)S(6)} %select_n.80, bf16[2,128,1024]{2,1,0:T(8,128)(2,1)S(1)} %copy-done.1, s32[]{:T(128)S(6)} %select_n.81), kind=kOutput, calls=%fused_computation.10 | convolution fusion | flops 943194112 | bytes 8519688 | tf_op jit(solution)/shard_map/dot_general | solution.py:421
  114.8 6.3 %bitcast_dynamic-update-slice_fusion.3 = bf16[5,1024,3584]{2,1,0:T(8,128)(2,1)} fusion(bf16[5,1024,3584]{2,1,0:T(8,128)(2,1)} %bitcast_dynamic-update-slice_fusion.4, bf16[4,128,3584]{2,1,0:T(8,128)(2,1)} %bitcast.142, s32[]{:T(128)S(6)} %select_n.84, bf16[2,128,1024]{2,1,0:T(8,128)(2,1)S(1)} %copy-done.1, s32[]{:T(128)S(6)} %select_n.82), kind=kOutput, calls=%fused_computation.9 | convolution fusion | flops 943194112 | bytes 8519688 | tf_op jit(solution)/shard_map/dot_general | solution.py:421
  121.1 6.3 %bitcast_dynamic-update-slice_fusion.2 = bf16[5,1024,3584]{2,1,0:T(8,128)(2,1)} fusion(bf16[5,1024,3584]{2,1,0:T(8,128)(2,1)} %bitcast_dynamic-update-slice_fusion.3, bf16[4,128,3584]{2,1,0:T(8,128)(2,1)} %bitcast.143, s32[]{:T(128)S(6)} %select_n.87, bf16[2,128,1024]{2,1,0:T(8,128)(2,1)S(1)} %copy-done.1, s32[]{:T(128)S(6)} %select_n.85), kind=kOutput, calls=%fused_computation.8 | convolution fusion | flops 943194112 | bytes 8519688 | tf_op jit(solution)/shard_map/dot_general | solution.py:421
  127.4 6.3 %bitcast_dynamic-update-slice_fusion.1 = bf16[5,1024,3584]{2,1,0:T(8,128)(2,1)} fusion(bf16[5,1024,3584]{2,1,0:T(8,128)(2,1)} %bitcast_dynamic-update-slice_fusion.2, bf16[4,128,3584]{2,1,0:T(8,128)(2,1)} %bitcast.144, s32[]{:T(128)S(6)} %select_n.90, bf16[2,128,1024]{2,1,0:T(8,128)(2,1)S(1)} %copy-done.1, s32[]{:T(128)S(6)} %select_n.88), kind=kOutput, calls=%fused_computation.7 | convolution fusion | flops 943194112 | bytes 8519688 | tf_op jit(solution)/shard_map/dot_general | solution.py:421
  133.7 0.0 copy-start.3
  133.7 6.5 %bitcast_dynamic-update-slice_fusion = bf16[5,1024,3584]{2,1,0:T(8,128)(2,1)} fusion(bf16[5,1024,3584]{2,1,0:T(8,128)(2,1)} %bitcast_dynamic-update-slice_fusion.1, bf16[4,128,3584]{2,1,0:T(8,128)(2,1)} %bitcast.145, s32[]{:T(128)S(6)} %select_n.93, bf16[2,128,1024]{2,1,0:T(8,128)(2,1)S(1)} %copy-done.1, s32[]{:T(128)S(6)} %select_n.91), kind=kOutput, calls=%fused_computation.6 | convolution fusion | flops 943194112 | bytes 8519688 | tf_op jit(solution)/shard_map/dot_general | solution.py:421
  140.2 0.1 broadcast.13
  140.3 0.0 copy-done.3
  140.3 5.7 %fusion.19 = f32[2,128,1024]{2,1,0:T(8,128)S(1)} fusion(f32[2,128,1024]{2,1,0:T(8,128)S(1)} %broadcast.13, s32[]{:T(128)S(6)} %select_n.81, bf16[5,1024,3584]{2,1,0:T(8,128)(2,1)} %dec_ref.1, bf16[4,128,3584]{2,1,0:T(8,128)(2,1)S(1)} %bitcast.146, s32[]{:T(128)S(6)} %select_n.80), kind=kOutput, calls=%fused_computation.30 | convolution fusion | flops 939524096 | bytes 8781832 | tf_op jit(solution)/shard_map/dot_general | solution.py:428
  146.1 5.5 %fusion.28 = f32[2,128,1024]{2,1,0:T(8,128)S(1)} fusion(f32[2,128,1024]{2,1,0:T(8,128)S(1)} %fusion.19, s32[]{:T(128)S(6)} %select_n.82, bf16[5,1024,3584]{2,1,0:T(8,128)(2,1)} %dec_ref.1, bf16[4,128,3584]{2,1,0:T(8,128)(2,1)S(1)} %bitcast.147, s32[]{:T(128)S(6)} %select_n.84, f32[1,128,1024]{2,1,0:T(8,128)S(1)} %constant_dynamic-slice_fusion.3), kind=kOutput, calls=%fused_computation.33 | convolution fusion | flops 939655168 | bytes 9306120 | tf_op jit(solution)/shard_map/dot_general | solution.py:428
  151.7 5.5 %fusion.37 = f32[2,128,1024]{2,1,0:T(8,128)S(1)} fusion(f32[2,128,1024]{2,1,0:T(8,128)S(1)} %fusion.28, s32[]{:T(128)S(6)} %select_n.85, bf16[5,1024,3584]{2,1,0:T(8,128)(2,1)} %dec_ref.1, bf16[4,128,3584]{2,1,0:T(8,128)(2,1)S(1)} %bitcast.148, s32[]{:T(128)S(6)} %select_n.87, f32[1,128,1024]{2,1,0:T(8,128)S(1)} %constant_dynamic-slice_fusion.2), kind=kOutput, calls=%fused_computation.36 | convolution fusion | flops 939655168 | bytes 9306120 | tf_op jit(solution)/shard_map/dot_general | solution.py:428
  157.3 5.5 %fusion.46 = f32[2,128,1024]{2,1,0:T(8,128)S(1)} fusion(f32[2,128,1024]{2,1,0:T(8,128)S(1)} %fusion.37, s32[]{:T(128)S(6)} %select_n.88, bf16[5,1024,3584]{2,1,0:T(8,128)(2,1)} %dec_ref.1, bf16[4,128,3584]{2,1,0:T(8,128)(2,1)S(1)} %bitcast.149, s32[]{:T(128)S(6)} %select_n.90, f32[1,128,1024]{2,1,0:T(8,128)S(1)} %constant_dynamic-slice_fusion.1), kind=kOutput, calls=%fused_computation.39 | convolution fusion | flops 939655168 | bytes 9306120 | tf_op jit(solution)/shard_map/dot_general | solution.py:428
  162.8 0.0 copy-start.2
  162.9 5.6 %fusion.55 = f32[2,128,1024]{2,1,0:T(8,128)S(1)} fusion(f32[2,128,1024]{2,1,0:T(8,128)S(1)} %fusion.46, s32[]{:T(128)S(6)} %select_n.91, bf16[5,1024,3584]{2,1,0:T(8,128)(2,1)} %dec_ref.1, bf16[4,128,3584]{2,1,0:T(8,128)(2,1)S(1)} %bitcast.150, s32[]{:T(128)S(6)} %select_n.93, f32[1,128,1024]{2,1,0:T(8,128)S(1)} %constant_dynamic-slice_fusion), kind=kOutput, calls=%fused_computation.42 | convolution fusion | flops 939655168 | bytes 9306120 | tf_op jit(solution)/shard_map/dot_general | solution.py:428
  168.5 0.0 copy-done.2
  168.5 1.0 convert_reduce_fusion
  169.5 7.3 %convert_bitcast_fusion = bf16[2,3584,1024]{1,2,0:T(8,128)(2,1)} fusion(bf16[2,128,1024]{2,1,0:T(8,128)(2,1)S(1)} %get-tuple-element.19, bf16[2,128,3584]{2,1,0:T(8,128)(2,1)S(1)} %bitcast.139), kind=kOutput, calls=%fused_computation | convolution fusion | flops 1886388224 | bytes 17039360 | tf_op jit(solution)/shard_map/krd,krf->kdf/dot_general | solution.py:438
  176.8 0.0 copy-start.4
  176.8 19.4 %copy.13 = bf16[2,3584,1024]{2,1,0:T(8,128)(2,1)} copy(bf16[2,3584,1024]{1,2,0:T(8,128)(2,1)} %convert_bitcast_fusion) | data formatting | bytes 29360128
  196.2 0.0 copy-done.4
  196.2 0.6 copy.26
  (9 shorter events, 0.3 us)
Async XLA Ops:
  0.6 22.1 %copy-start.5 = (f32[2,1024]{1,0:T(2,128)S(1)}, f32[2,1024]{1,0:T(2,128)}, u32[]{:S(2)}) copy-start(f32[2,1024]{1,0:T(2,128)} %param.9) | copy-start | bytes 24580
  2.2 1.2 copy-start
  31.2 77.2 %copy-start.1 = (bf16[2,128,1024]{2,1,0:T(8,128)(2,1)S(1)}, bf16[2,128,1024]{2,1,0:T(8,128)(2,1)}, u32[]{:S(2)}) copy-start(bf16[2,128,1024]{2,1,0:T(8,128)(2,1)} %get-tuple-element.22.codes_ref) | copy-start | bytes 1572868
  133.7 6.6 %copy-start.3 = (bf16[4,8,16,3584]{3,2,1,0:T(8,128)(2,1)S(1)}, bf16[4,8,16,3584]{3,2,1,0:T(8,128)(2,1)}, u32[]{:S(2)}) copy-start(bf16[4,8,16,3584]{3,2,1,0:T(8,128)(2,1)} %get-tuple-element.7) | copy-start | bytes 11010052
  162.8 5.7 %copy-start.2 = (f32[2,128,1024]{2,1,0:T(8,128)S(1)}, f32[2,128,1024]{2,1,0:T(8,128)}, u32[]{:S(2)}) copy-start(f32[2,128,1024]{2,1,0:T(8,128)} %get-tuple-element.23) | copy-start | bytes 3145732
  176.8 19.4 %copy-start.4 = (bf16[4,4,3584]{2,1,0:T(4,128)(2,1)S(1)}, bf16[4,4,3584]{2,1,0:T(4,128)(2,1)}, u32[]{:S(2)}) copy-start(bf16[4,4,3584]{2,1,0:T(4,128)(2,1)} %get-tuple-element.28) | copy-start | bytes 344068

commit v2 on v1

--- a/solution.py
+++ b/solution.py
@@ -138,7 +138,7 @@
 
 
 def exchange_kernel(
-    layer_count, dp_count, codes_ref, dec_ref, target_ref, recon_ref, err_out,
+    layer_count, dp_count, codes_ref, dec_ref, target_ref, recon_ref, err_out, back_ref,
     weights, part, arrivals, err, zsend, zrecv, zall, acc,
     load_sem, rs_send, rs_recv, z_send, z_recv, g_send, g_recv, ag_send, ag_recv, out_sem,
 ):
@@ -149,10 +149,14 @@
     rows = part.shape[2]
     share = target_ref.shape[1]
     f32, bf16 = jnp.float32, jnp.bfloat16
-    loads = []
-    for pair in range(pairs):
-        loads.append(pltpu.make_async_copy(dec_ref.at[pair], weights.at[pair], load_sem.at[pair]))
-        loads[-1].start()
+
+    def load(pair):
+        return pltpu.make_async_copy(dec_ref.at[pair], weights.at[pair], load_sem.at[pair])
+
+    for pair in range(LAYERS - 1):
+        load(pair).start()
+    for pair in range(LAYERS - 1, pairs):
+        load(pair).start()
     barrier, greeted = greet(layer, dp, dp_count, range(nbits))
     tile = 512 if width % 512 == 0 else 128
     orders = []
@@ -162,6 +166,8 @@
     copies = {}
 
     def add_pair(slot, pair, fresh):
+        load(pair).wait()
+
         def body(step, carry):
             columns = pl.ds(pl.multiple_of(step * tile, tile), tile)
             value = jnp.dot(
@@ -175,12 +181,40 @@
 
         lax.fori_loop(0, width // tile, body, 0)
 
-    def wait_load(pair):
-        loads[pair].wait()
+    def pull_pair(target, slot, pair, fresh):
+        deep = min(256, weights.shape[1])
+
+        def body(step, carry):
+            features = pl.ds(pl.multiple_of(step * deep, deep), deep)
+            value = lax.dot_general(
+                err[target].reshape(acc.shape),
+                weights[pair, features, :],
+                (((1,), (1,)), ((), ())),
+                preferred_element_type=f32,
+            )
+            if fresh:
+                back_ref[slot, :, features] = value
+            else:
+                back_ref[slot, :, features] += value
+            return carry
+
+        lax.fori_loop(0, weights.shape[1] // deep, body, 0)
+
+    def pull(target):
+        if target == 0:
+            pl.when(side == 0)(lambda: pull_pair(0, 0, 0, True))
+        elif target == 1:
+            pl.when(side == 0)(lambda: pull_pair(1, 0, 1, False))
+            pl.when(side == 1)(lambda: pull_pair(1, 0, 0, True))
+        else:
+            pull_pair(target, 0, target - side, False)
+        if target == LAYERS - 2:
+            pl.when(side == 1)(lambda: pull_pair(target, 1, target + 1, True))
+        elif target == LAYERS - 1:
+            pl.when(side == 1)(lambda: pull_pair(target, 1, target + 1, False))
+            pl.when(side == 0)(lambda: pull_pair(target, 1, target + 1, True))
 
     def decode(target):
-        has_first = (target >= side) if target == 0 else None
-
         def first():
             add_pair(0, target - side, True)
 
@@ -310,13 +344,13 @@
                 copy.start()
                 copies["out", target, 0] = copy
 
-    for load in loads:
-        load.wait()
     last = 2 * nbits + 2
     for wave in range(last + LAYERS):
         for target in range(LAYERS - 1, -1, -1):
             if 0 <= wave - target <= last:
                 run(target, wave - target)
+        if 0 <= wave - last < LAYERS:
+            pull(wave - last)
     for key, copy in copies.items():
         if key[0] == "out":
             copy.wait()
@@ -331,11 +365,12 @@
     share = rows // dp_count
     bf16 = jnp.bfloat16
     dma = pltpu.SemaphoreType.DMA
-    recon, errors = pl.pallas_call(
+    recon, errors, back = pl.pallas_call(
         functools.partial(exchange_kernel, layer_count, dp_count),
         out_shape=[
             jax.ShapeDtypeStruct((LAYERS, share, width), bf16),
             jax.ShapeDtypeStruct((LAYERS, layer_count, rows, width), bf16),
+            jax.ShapeDtypeStruct((2, tokens, local_width), jnp.float32),
         ],
         in_specs=[
             pl.BlockSpec(memory_space=pltpu.VMEM),
@@ -345,6 +380,7 @@
         out_specs=[
             pl.BlockSpec(memory_space=pltpu.VMEM),
             pl.BlockSpec(memory_space=pl.ANY),
+            pl.BlockSpec(memory_space=pltpu.VMEM),
         ],
         scratch_shapes=[
             pltpu.VMEM((pairs, local_width, width), bf16),
@@ -371,7 +407,74 @@
         ),
         name="decode_exchange",
     )(codes, decoder, targets)
-    return recon, errors.reshape(LAYERS, tokens, width)
+    return recon, errors.reshape(LAYERS, tokens, width), back
+
+
+def grad_decoder_kernel(source_ref, target_ref, codes_ref, err_ref, out_ref):
+    width = err_ref.shape[2]
+    tile = 512 if width % 512 == 0 else 128
+    for first in range(0, width, tile):
+        out_ref[0, :, first:first + tile] = lax.dot_general(
+            codes_ref[0],
+            err_ref[0, :, first:first + tile],
+            (((0,), (0,)), ((), ())),
+            preferred_element_type=jnp.float32,
+        ).astype(out_ref.dtype)
+
+
+def decoder_grad(codes, errors, sources, targets, pairs):
+    tokens, local_width = codes.shape[1:]
+    width = errors.shape[2]
+    deep = min(256, local_width)
+    return pl.pallas_call(
+        grad_decoder_kernel,
+        out_shape=jax.ShapeDtypeStruct((pairs, local_width, width), jnp.bfloat16),
+        grid_spec=pltpu.PrefetchScalarGridSpec(
+            num_scalar_prefetch=2,
+            grid=(pairs, local_width // deep),
+            in_specs=[
+                pl.BlockSpec((1, tokens, deep), lambda p, f, src, tgt: (src[p], 0, f)),
+                pl.BlockSpec((1, tokens, width), lambda p, f, src, tgt: (tgt[p], 0, 0)),
+            ],
+            out_specs=pl.BlockSpec((1, deep, width), lambda p, f, src, tgt: (p, f, 0)),
+        ),
+        name="decoder_grad",
+    )(sources, targets, codes, errors)
+
+
+def grad_encoder_kernel(x_ref, back_ref, keep_ref, positive_ref, grad_ref, bias_ref, back_pre):
+    @pl.when(pl.program_id(1) == 0)
+    def _():
+        value = (back_ref[0] * keep_ref[0] * (2.0 * positive_ref[0])).astype(jnp.bfloat16)
+        back_pre[...] = value
+        bias_ref[0] = jnp.sum(value.astype(jnp.float32), axis=0, keepdims=True)
+
+    grad_ref[0] = lax.dot_general(
+        x_ref[0], back_pre[...], (((0,), (0,)), ((), ())), preferred_element_type=jnp.float32
+    ).astype(grad_ref.dtype)
+
+
+def encoder_grad(inputs, back, keep, positive):
+    slots, tokens, width = inputs.shape
+    local_width = back.shape[2]
+    tile = 512 if width % 512 == 0 else 128
+    whole = pl.BlockSpec((1, tokens, local_width), lambda k, d: (k, 0, 0))
+    grad, bias = pl.pallas_call(
+        grad_encoder_kernel,
+        out_shape=[
+            jax.ShapeDtypeStruct((slots, width, local_width), jnp.bfloat16),
+            jax.ShapeDtypeStruct((slots, 1, local_width), jnp.float32),
+        ],
+        grid=(slots, width // tile),
+        in_specs=[pl.BlockSpec((1, tokens, tile), lambda k, d: (k, 0, d)), whole, whole, whole],
+        out_specs=[
+            pl.BlockSpec((1, tile, local_width), lambda k, d: (k, d, 0)),
+            pl.BlockSpec((1, 1, local_width), lambda k, d: (k, 0, 0)),
+        ],
+        scratch_shapes=[pltpu.VMEM((tokens, local_width), jnp.bfloat16)],
+        name="encoder_grad",
+    )(inputs, back, keep, positive)
+    return grad, bias.reshape(slots, local_width)
 
 
 def per_device(resid_in, resid_out, encoder, enc_bias, decoder, active):
@@ -404,41 +507,17 @@
     block_keep = jnp.stack(block_masks)
     positive = jnp.maximum(pre_acts, 0.0)
     feature_codes = (block_keep * positive * positive).astype(jnp.bfloat16)
-    recon, errors_all = exchange(feature_codes, decoder, resid_out, layer_count, dp_count)
-    pair_table = []
-    for pair_slot in range(decoder.shape[0]):
-        second = pair_slot >= LAYERS - fold_side
-        pair_table.append(
-            (second.astype(jnp.int32), jnp.where(second, pair_slot - 1, fold_side + pair_slot))
-        )
-    grad_parts = []
-    back_codes = jnp.zeros((2, tokens, local_width), jnp.float32)
-    for pair_slot in range(decoder.shape[0]):
-        source_slot, target_layer = pair_table[pair_slot]
-        source_codes = lax.dynamic_index_in_dim(feature_codes, source_slot, 0, keepdims=False)
-        target_errors = lax.dynamic_index_in_dim(errors_all, target_layer, 0, keepdims=False)
-        grad_parts.append(
-            lax.dot_general(
-                source_codes,
-                target_errors,
-                (((0,), (0,)), ((), ())),
-                preferred_element_type=jnp.float32,
-            ).astype(jnp.bfloat16)
-        )
-        pulled = lax.dot_general(
-            target_errors,
-            decoder[pair_slot],
-            (((1,), (1,)), ((), ())),
-            preferred_element_type=jnp.float32,
-        )
-        current = lax.dynamic_index_in_dim(back_codes, source_slot, 0, keepdims=False)
-        back_codes = lax.dynamic_update_index_in_dim(back_codes, current + pulled, source_slot, 0)
-    grad_decoder = jnp.stack(grad_parts)
-    back_pre = (back_codes * block_keep * (2.0 * positive)).astype(jnp.bfloat16)
-    grad_encoder = jnp.einsum(
-        "krd,krf->kdf", inputs, back_pre, preferred_element_type=jnp.float32
-    ).astype(jnp.bfloat16)
-    grad_bias = jnp.sum(back_pre.astype(jnp.float32), axis=1)
+    recon, errors_all, back_codes = exchange(
+        feature_codes, decoder, resid_out, layer_count, dp_count
+    )
+    pair_slots = jnp.arange(decoder.shape[0], dtype=jnp.int32)
+    second = pair_slots >= LAYERS - fold_side
+    sources = second.astype(jnp.int32)
+    decoded_into = jnp.where(second, pair_slots - 1, fold_side + pair_slots).astype(jnp.int32)
+    grad_decoder = decoder_grad(
+        feature_codes, errors_all, sources, decoded_into, decoder.shape[0]
+    )
+    grad_encoder, grad_bias = encoder_grad(inputs, back_codes, block_keep, positive)
     return (recon, grad_encoder, grad_bias, grad_decoder)
 
 

time: 199 us -> 157 us (0.79)
  matrix products: 75.6 us -> 9.42 us
  Pallas kernels: 96.4 us -> 140 us
  local copies, waits for them, and re-layouts: 22.7 us -> 4.29 us
    dot_general x11 -> x0, matrix products: 67 us -> none  [the longest x5 31.8 us: per_device(): lax.dot_general(source_codes, target_errors, (((0,), (0,)), ((), ())), pr...]
    pallas_call x0 -> x2, Pallas kernels: none -> 39.5 us  [the longest x1 25.1 us: decoder_grad(): pl.pallas_call(grad_decoder_kernel, out_shape=jax.ShapeDtypeStruct((pairs...]
    unnamed x15 -> x11, local copies, waits for them, and re-layouts: 21.3 us -> 3.17 us
    pallas_call x1, Pallas kernels: 77.1 us -> 81 us  [exchange(): pl.pallas_call(functools.partial(exchange_kernel, layer_count, dp_count),...]
where the time goes in v2:
time: 157 us; the launch traced here: 156 us
  Pallas kernels  140 us (89%)
  matrix products  9.42 us (6%)
  local copies, waits for them, and re-layouts  4.29 us (3%)
    pallas_call x1, Pallas kernels, exchange(): pl.pallas_call(functools.partial(exchange_kernel, layer_count, dp_count),...  81 us
    pallas_call x1, Pallas kernels, decoder_grad(): pl.pallas_call(grad_decoder_kernel, out_shape=jax.ShapeDtypeStruct((pairs...  25.1 us
    pallas_call x1, Pallas kernels, gather_inputs(): pl.pallas_call(functools.partial(gather_kernel, layer_count, dp_count), o...  19.3 us
    pallas_call x1, Pallas kernels, encoder_grad(): pl.pallas_call(grad_encoder_kernel, out_shape=[jax.ShapeDtypeStruct((slot...  14.4 us
    dot_general x1, matrix products, per_device(): jnp.einsum('krd,kdf->krf', inputs, encoder, preferred_element_type=jnp.fl...  9.42 us
    unnamed x11, local copies, waits for them, and re-layouts  3.17 us

profile of v2, /device:TPU:12, one launch (start us, length us, event | category | flops | bytes accessed | tf_op | source)
XLA Modules:
  0.0 155.6 jit_solution(11676151690909694256)
XLA Ops:
  0.7 0.5 compare_select_fusion.target_ref
  1.2 0.5 compare_convert_fusion.source_ref
  1.7 0.7 dynamic-slice_bitcast_fusion.1
  2.4 0.3 compare_reduce_fusion
  2.7 0.1 broadcast_in_dim.4
  2.8 0.1 stack_reshape.6
  2.9 0.1 broadcast_in_dim.5
  3.0 0.1 stack_reshape.7
  3.2 0.0 copy-start.1
  3.2 1.2 copy-done.1
  4.4 0.0 copy-start.2
  4.4 19.3 %gather_inputs.1 = bf16[2,4,2,16,3584]{4,3,2,1,0:T(8,128)(2,1)S(1)} custom-call(bf16[4,2,16,3584]{3,2,1,0:T(8,128)(2,1)S(1)} %bitcast.18), custom_call_target="tpu_custom_call" | custom-call | tf_op jit(solution)/shard_map/gather_inputs/pallas_call | solution.py:120
  23.7 0.0 copy-start
  23.7 9.4 %fusion.1 = (bf16[2,128,1024]{2,1,0:T(8,128)(2,1)}, f32[2,128,1024]{2,1,0:T(8,128)}) fusion(f32[2,128,1024]{2,1,0:T(8,128)S(1)} %constant_dynamic-update-slice_fusion.keep_ref, f32[2,1024]{1,0:T(2,128)} %param.9, bf16[2,128,3584]{2,1,0:T(8,128)(2,1)S(1)} %bitcast.16, bf16[2,3584,1024]{2,1,0:T(8,128)(2,1)} %param.8), kind=kOutput, calls=%fused_computation.3 | convolution fusion | flops 1880358912 | bytes 19144704 | tf_op jit(solution)/shard_map/krd,kdf->krf/dot_general | solution.py:493
  33.1 0.0 copy-done.2
  33.1 81.0 %decode_exchange.1 = (bf16[4,4,3584]{2,1,0:T(4,128)(2,1)}, bf16[4,8,16,3584]{3,2,1,0:T(8,128)(2,1)}, f32[2,128,1024]{2,1,0:T(8,128)}) custom-call(bf16[2,128,1024]{2,1,0:T(8,128)(2,1)} %get-tuple-element.18.codes_ref, bf16[5,1024,3584]{2,1,0:T(8,128)(2,1)} %dec_ref.1, bf16[4,4,3584]{2,1,0:T(4,128)(2,1)} %target_ref.1), custom_call_target="tpu_custom_call" | custom-call | tf_op jit(solution)/shard_map/decode_exchange/pallas_call | solution.py:368
  114.1 0.0 copy-done
  114.1 14.4 %encoder_grad.1 = (bf16[2,3584,1024]{2,1,0:T(8,128)(2,1)}, f32[2,1,1024]{2,1,0:T(1,128)}) custom-call(bf16[2,128,3584]{2,1,0:T(8,128)(2,1)} %bitcast.17, f32[2,128,1024]{2,1,0:T(8,128)} %get-tuple-element.10.back_ref, f32[2,128,1024]{2,1,0:T(8,128)} %copy-done.2, f32[2,128,1024]{2,1,0:T(8,128)} %get-tuple-element.19.positive_ref), custom_call_target="tpu_custom_call" | custom-call | tf_op jit(solution)/shard_map/encoder_grad/pallas_call | solution.py:462
  128.6 1.3 copy.12
  129.9 0.0 copy-start.3
  129.9 25.1 %decoder_grad.1 = bf16[5,1024,3584]{2,1,0:T(8,128)(2,1)} custom-call(s32[5]{0:T(128)} %compare_convert_fusion.source_ref, s32[5]{0:T(128)} %compare_select_fusion.target_ref, bf16[2,128,1024]{2,1,0:T(8,128)(2,1)} %get-tuple-element.18.codes_ref, bf16[4,128,3584]{2,1,0:T(8,128)(2,1)} %bitcast.19), custom_call_target="tpu_custom_call" | custom-call | tf_op jit(solution)/shard_map/decoder_grad/pallas_call | solution.py:429
  154.9 0.0 copy-done.3
  154.9 0.6 copy.15
  (5 shorter events, 0.1 us)
Async XLA Ops:
  3.2 1.2 copy-start.1
  4.4 28.7 %copy-start.2 = (f32[2,128,1024]{2,1,0:T(8,128)}, f32[2,128,1024]{2,1,0:T(8,128)S(1)}, u32[]{:S(2)}) copy-start(f32[2,128,1024]{2,1,0:T(8,128)S(1)} %constant_dynamic-update-slice_fusion.keep_ref) | copy-start | bytes 3145732
  23.7 90.4 %copy-start = (bf16[2,4,2,16,3584]{4,3,2,1,0:T(8,128)(2,1)}, bf16[2,4,2,16,3584]{4,3,2,1,0:T(8,128)(2,1)S(1)}, u32[]{:S(2)}) copy-start(bf16[2,4,2,16,3584]{4,3,2,1,0:T(8,128)(2,1)S(1)} %gather_inputs.1) | copy-start | bytes 5505028
  129.9 25.1 %copy-start.3 = (bf16[4,4,3584]{2,1,0:T(4,128)(2,1)S(1)}, bf16[4,4,3584]{2,1,0:T(4,128)(2,1)}, u32[]{:S(2)}) copy-start(bf16[4,4,3584]{2,1,0:T(4,128)(2,1)} %get-tuple-element.24) | copy-start | bytes 344068

commit v3 on v2

--- a/solution.py
+++ b/solution.py
@@ -410,71 +410,88 @@
     return recon, errors.reshape(LAYERS, tokens, width), back
 
 
-def grad_decoder_kernel(source_ref, target_ref, codes_ref, err_ref, out_ref):
+def half_width(width):
+    return width // 2 if width % 256 == 0 else width
+
+
+def grad_decoder_kernel(side_ref, codes_ref, err_ref, out_ref, turned):
+    @pl.when(pl.program_id(1) == 0)
+    def _():
+        turned[...] = codes_ref[0].T
+
     width = err_ref.shape[2]
-    tile = 512 if width % 512 == 0 else 128
+    tile = 256 if width % 256 == 0 else 128
     for first in range(0, width, tile):
-        out_ref[0, :, first:first + tile] = lax.dot_general(
-            codes_ref[0],
-            err_ref[0, :, first:first + tile],
-            (((0,), (0,)), ((), ())),
-            preferred_element_type=jnp.float32,
+        out_ref[0, :, first:first + tile] = jnp.dot(
+            turned[...], err_ref[0, :, first:first + tile], preferred_element_type=jnp.float32
         ).astype(out_ref.dtype)
 
 
-def decoder_grad(codes, errors, sources, targets, pairs):
+def decoder_grad(codes, errors, side, pairs):
     tokens, local_width = codes.shape[1:]
     width = errors.shape[2]
-    deep = min(256, local_width)
+    block = half_width(width)
+
+    def source(pair, side_ref):
+        return (pair + side_ref[0]) // LAYERS
+
+    def target(pair, side_ref):
+        return pair + side_ref[0] - source(pair, side_ref) * (1 + side_ref[0])
+
     return pl.pallas_call(
         grad_decoder_kernel,
         out_shape=jax.ShapeDtypeStruct((pairs, local_width, width), jnp.bfloat16),
         grid_spec=pltpu.PrefetchScalarGridSpec(
-            num_scalar_prefetch=2,
-            grid=(pairs, local_width // deep),
+            num_scalar_prefetch=1,
+            grid=(pairs, width // block),
             in_specs=[
-                pl.BlockSpec((1, tokens, deep), lambda p, f, src, tgt: (src[p], 0, f)),
-                pl.BlockSpec((1, tokens, width), lambda p, f, src, tgt: (tgt[p], 0, 0)),
+                pl.BlockSpec((1, tokens, local_width), lambda p, d, s: (source(p, s), 0, 0)),
+                pl.BlockSpec((1, tokens, block), lambda p, d, s: (target(p, s), 0, d)),
             ],
-            out_specs=pl.BlockSpec((1, deep, width), lambda p, f, src, tgt: (p, f, 0)),
+            out_specs=pl.BlockSpec((1, local_width, block), lambda p, d, s: (p, 0, d)),
+            scratch_shapes=[pltpu.VMEM((local_width, tokens), codes.dtype)],
         ),
         name="decoder_grad",
-    )(sources, targets, codes, errors)
+    )(side, codes, errors)
 
 
 def grad_encoder_kernel(x_ref, back_ref, keep_ref, positive_ref, grad_ref, bias_ref, back_pre):
+    slot = pl.program_id(0)
+
     @pl.when(pl.program_id(1) == 0)
     def _():
         value = (back_ref[0] * keep_ref[0] * (2.0 * positive_ref[0])).astype(jnp.bfloat16)
         back_pre[...] = value
-        bias_ref[0] = jnp.sum(value.astype(jnp.float32), axis=0, keepdims=True)
-
-    grad_ref[0] = lax.dot_general(
-        x_ref[0], back_pre[...], (((0,), (0,)), ((), ())), preferred_element_type=jnp.float32
-    ).astype(grad_ref.dtype)
+        bias_ref[pl.ds(slot, 1), :] = jnp.sum(value.astype(jnp.float32), axis=0, keepdims=True)
+
+    turned = x_ref[0].T
+    tile = min(256, back_pre.shape[1])
+    for first in range(0, back_pre.shape[1], tile):
+        grad_ref[0, :, first:first + tile] = jnp.dot(
+            turned, back_pre[:, first:first + tile], preferred_element_type=jnp.float32
+        ).astype(grad_ref.dtype)
 
 
 def encoder_grad(inputs, back, keep, positive):
     slots, tokens, width = inputs.shape
     local_width = back.shape[2]
-    tile = 512 if width % 512 == 0 else 128
+    block = half_width(width)
     whole = pl.BlockSpec((1, tokens, local_width), lambda k, d: (k, 0, 0))
-    grad, bias = pl.pallas_call(
+    return pl.pallas_call(
         grad_encoder_kernel,
         out_shape=[
             jax.ShapeDtypeStruct((slots, width, local_width), jnp.bfloat16),
-            jax.ShapeDtypeStruct((slots, 1, local_width), jnp.float32),
-        ],
-        grid=(slots, width // tile),
-        in_specs=[pl.BlockSpec((1, tokens, tile), lambda k, d: (k, 0, d)), whole, whole, whole],
+            jax.ShapeDtypeStruct((slots, local_width), jnp.float32),
+        ],
+        grid=(slots, width // block),
+        in_specs=[pl.BlockSpec((1, tokens, block), lambda k, d: (k, 0, d)), whole, whole, whole],
         out_specs=[
-            pl.BlockSpec((1, tile, local_width), lambda k, d: (k, d, 0)),
-            pl.BlockSpec((1, 1, local_width), lambda k, d: (k, 0, 0)),
+            pl.BlockSpec((1, block, local_width), lambda k, d: (k, d, 0)),
+            pl.BlockSpec((slots, local_width), lambda k, d: (0, 0)),
         ],
         scratch_shapes=[pltpu.VMEM((tokens, local_width), jnp.bfloat16)],
         name="encoder_grad",
     )(inputs, back, keep, positive)
-    return grad, bias.reshape(slots, local_width)
 
 
 def per_device(resid_in, resid_out, encoder, enc_bias, decoder, active):
@@ -510,13 +527,8 @@
     recon, errors_all, back_codes = exchange(
         feature_codes, decoder, resid_out, layer_count, dp_count
     )
-    pair_slots = jnp.arange(decoder.shape[0], dtype=jnp.int32)
-    second = pair_slots >= LAYERS - fold_side
-    sources = second.astype(jnp.int32)
-    decoded_into = jnp.where(second, pair_slots - 1, fold_side + pair_slots).astype(jnp.int32)
-    grad_decoder = decoder_grad(
-        feature_codes, errors_all, sources, decoded_into, decoder.shape[0]
-    )
+    side = fold_side.astype(jnp.int32).reshape(1)
+    grad_decoder = decoder_grad(feature_codes, errors_all, side, decoder.shape[0])
     grad_encoder, grad_bias = encoder_grad(inputs, back_codes, block_keep, positive)
     return (recon, grad_encoder, grad_bias, grad_decoder)
 

time: 157 us -> 142 us (0.904)
  Pallas kernels: 140 us -> 128 us
    pallas_call x1, Pallas kernels: 25.1 us -> 17.7 us  [decoder_grad(): pl.pallas_call(grad_decoder_kernel, out_shape=jax.ShapeDtypeStruct((pairs...]
    pallas_call x1, Pallas kernels: 14.4 us -> 10.1 us  [encoder_grad(): pl.pallas_call(grad_encoder_kernel, out_shape=[jax.ShapeDtypeStruct((slot...]
    unnamed x11 -> x10, local copies, waits for them, and re-layouts: 3.17 us -> 1.87 us
where the time goes in v3:
time: 142 us
  Pallas kernels  128 us (90%)
  matrix products  9.41 us (7%)
  local copies, waits for them, and re-layouts  3 us (2%)
    pallas_call x1, Pallas kernels, exchange(): pl.pallas_call(functools.partial(exchange_kernel, layer_count, dp_count),...  81.2 us
    pallas_call x1, Pallas kernels, gather_inputs(): pl.pallas_call(functools.partial(gather_kernel, layer_count, dp_count), o...  19.3 us
    pallas_call x1, Pallas kernels, decoder_grad(): pl.pallas_call(grad_decoder_kernel, out_shape=jax.ShapeDtypeStruct((pairs...  17.7 us
    pallas_call x1, Pallas kernels, encoder_grad(): pl.pallas_call(grad_encoder_kernel, out_shape=[jax.ShapeDtypeStruct((slot...  10.1 us
    dot_general x1, matrix products, per_device(): jnp.einsum('krd,kdf->krf', inputs, encoder, preferred_element_type=jnp.fl...  9.41 us

profile of v3, /device:TPU:12, one launch (start us, length us, event | category | flops | bytes accessed | tf_op | source)
XLA Modules:
  0.0 141.7 jit_solution(10624499421523403830)
XLA Ops:
  0.7 0.7 dynamic-slice_bitcast_fusion.1
  1.4 0.3 compare_reduce_fusion
  1.7 0.1 broadcast_in_dim.4
  1.8 0.1 stack_reshape.6
  1.9 0.1 broadcast_in_dim.5
  2.0 0.1 stack_reshape.7
  2.2 0.0 copy-start.1
  2.2 1.2 copy-done.1
  3.4 0.0 copy-start.2
  3.4 19.3 %gather_inputs.1 = bf16[2,4,2,16,3584]{4,3,2,1,0:T(8,128)(2,1)S(1)} custom-call(bf16[4,2,16,3584]{3,2,1,0:T(8,128)(2,1)S(1)} %bitcast.16), custom_call_target="tpu_custom_call" | custom-call | tf_op jit(solution)/shard_map/gather_inputs/pallas_call | solution.py:120
  22.7 0.0 copy-start
  22.7 9.4 %fusion.1 = (bf16[2,128,1024]{2,1,0:T(8,128)(2,1)}, f32[2,128,1024]{2,1,0:T(8,128)}) fusion(f32[2,128,1024]{2,1,0:T(8,128)S(1)} %constant_dynamic-update-slice_fusion.keep_ref, f32[2,1024]{1,0:T(2,128)} %param.9, bf16[2,128,3584]{2,1,0:T(8,128)(2,1)S(1)} %bitcast.14, bf16[2,3584,1024]{2,1,0:T(8,128)(2,1)} %param.8), kind=kOutput, calls=%fused_computation.3 | convolution fusion | flops 1880358912 | bytes 19144704 | tf_op jit(solution)/shard_map/krd,kdf->krf/dot_general | solution.py:510
  32.1 0.0 copy-done.2
  32.1 81.2 %decode_exchange.1 = (bf16[4,4,3584]{2,1,0:T(4,128)(2,1)}, bf16[4,8,16,3584]{3,2,1,0:T(8,128)(2,1)}, f32[2,128,1024]{2,1,0:T(8,128)}) custom-call(bf16[2,128,1024]{2,1,0:T(8,128)(2,1)} %get-tuple-element.18.codes_ref, bf16[5,1024,3584]{2,1,0:T(8,128)(2,1)} %dec_ref.1, bf16[4,4,3584]{2,1,0:T(4,128)(2,1)} %target_ref.1), custom_call_target="tpu_custom_call" | custom-call | tf_op jit(solution)/shard_map/decode_exchange/pallas_call | solution.py:368
  113.3 0.0 copy-done
  113.3 10.1 %encoder_grad.1 = (bf16[2,3584,1024]{2,1,0:T(8,128)(2,1)}, f32[2,1024]{1,0:T(2,128)}) custom-call(bf16[2,128,3584]{2,1,0:T(8,128)(2,1)} %bitcast.15, f32[2,128,1024]{2,1,0:T(8,128)} %get-tuple-element.10.back_ref, f32[2,128,1024]{2,1,0:T(8,128)} %copy-done.2, f32[2,128,1024]{2,1,0:T(8,128)} %get-tuple-element.19.positive_ref), custom_call_target="tpu_custom_call" | custom-call | tf_op jit(solution)/shard_map/encoder_grad/pallas_call | solution.py:480
  123.4 0.0 copy-start.3
  123.4 17.7 %decoder_grad.1 = bf16[5,1024,3584]{2,1,0:T(8,128)(2,1)} custom-call(s32[1]{0:T(128)} %bitcast.4.side_ref, bf16[2,128,1024]{2,1,0:T(8,128)(2,1)} %get-tuple-element.18.codes_ref, bf16[4,128,3584]{2,1,0:T(8,128)(2,1)} %bitcast.17), custom_call_target="tpu_custom_call" | custom-call | tf_op jit(solution)/shard_map/decoder_grad/pallas_call | solution.py:441
  141.1 0.0 copy-done.3
  141.1 0.6 copy.12
  (5 shorter events, 0.1 us)
Async XLA Ops:
  2.2 1.2 copy-start.1
  3.4 28.7 %copy-start.2 = (f32[2,128,1024]{2,1,0:T(8,128)}, f32[2,128,1024]{2,1,0:T(8,128)S(1)}, u32[]{:S(2)}) copy-start(f32[2,128,1024]{2,1,0:T(8,128)S(1)} %constant_dynamic-update-slice_fusion.keep_ref) | copy-start | bytes 3145732
  22.7 90.6 %copy-start = (bf16[2,4,2,16,3584]{4,3,2,1,0:T(8,128)(2,1)}, bf16[2,4,2,16,3584]{4,3,2,1,0:T(8,128)(2,1)S(1)}, u32[]{:S(2)}) copy-start(bf16[2,4,2,16,3584]{4,3,2,1,0:T(8,128)(2,1)S(1)} %gather_inputs.1) | copy-start | bytes 5505028
  123.4 17.7 %copy-start.3 = (bf16[4,4,3584]{2,1,0:T(4,128)(2,1)S(1)}, bf16[4,4,3584]{2,1,0:T(4,128)(2,1)}, u32[]{:S(2)}) copy-start(bf16[4,4,3584]{2,1,0:T(4,128)(2,1)} %get-tuple-element.24) | copy-start | bytes 344068
